TPU v7x, 32 devices: a whole 2x2x4 slice. The times are simulated.
32 devices in a mesh: groups: 2 (over y), shard: 4 (over z), sub: 2 (over x), chan: 2 (over core).
Axes of the slice: x: 2, y: 2, z: 4, core: 2. Of those that a mesh axis runs over, the one named last changes fastest.
Arguments:
- field: bfloat16 [32, 8, 96, 128], P(('groups', 'shard'), 'sub', 'chan'), parts along dimension 0, may hold values from -6 to 6
- cotangent: bfloat16 [32, 8, 96, 128], P(('groups', 'shard'), 'sub', 'chan'), parts along dimension 0, may hold values from -6 to 6
- space_weight: bfloat16 [3, 3, 96, 96], replicated, may hold values from -0.21875 to 0.21875
- time_weight: bfloat16 [9, 96], P(None, 'chan'), may hold values from -2 to 2
Outputs:
- output: bfloat16 [32, 8, 96, 128], P(('groups', 'shard'), 'sub', 'chan'), parts along dimension 0
- field_grad: bfloat16 [32, 8, 96, 128], P(('groups', 'shard'), 'sub', 'chan'), parts along dimension 0
- space_grad: float32 [6, 3, 96, 96], P('groups', None, 'chan'), parts along dimension 0
- time_grad: float32 [18, 96], P('groups', 'chan'), parts along dimension 0
There are 2 independent parts, one for each index of `groups`. A program takes and returns all parts, laid end to end along the dimension named above; an argument that names none is the same for every part. Nothing has to cross between parts.
All inputs are finite; a program needn't handle non-finite values.
Results may differ from a plain program's by a relative error of at most 0.0048.
Values may be sent and summed in bfloat16 or wider, within the bound.
A program may use at most 64 MiB of HBM per device.

v0:
```python
import jax
import jax.numpy as jnp
from jax import lax
from jax.sharding import PartitionSpec as P


def with_halo(cells, sides, width):
    for axis, dim in sides:
        count = lax.axis_size(axis)
        ends = count - 1
        head = lax.slice_in_dim(cells, 0, width, axis=dim)
        tail = lax.slice_in_dim(cells, cells.shape[dim] - width, cells.shape[dim], axis=dim)
        cells = jnp.concatenate(
            [
                lax.ppermute(tail, axis, [(i, (i + 1) % count) for i in range(ends)]),
                cells,
                lax.ppermute(head, axis, [((i + 1) % count, i) for i in range(ends)]),
            ],
            axis=dim,
        )
    return cells


def gelu_tanh(values):
    return jax.nn.gelu(values, approximate=True)


def widen(values):
    rimmed = with_halo(values, (("sub", 1),), 1)
    gathered = lax.all_gather(rimmed, "chan", axis=2, tiled=True)
    return jnp.pad(gathered, ((0, 0), (0, 0), (0, 0), (1, 1)))


def to_time(values):
    return lax.all_to_all(values, "shard", split_axis=1, concat_axis=0, tiled=True)


def to_space(values):
    return lax.all_to_all(values, "shard", split_axis=0, concat_axis=1, tiled=True)


def pad_time(values):
    return jnp.pad(values, ((4, 4), (0, 0), (0, 0), (0, 0)))


def time_forward(padded, taps, count):
    total = jnp.zeros((count,) + padded.shape[1:], jnp.float32)
    for k in range(9):
        total = total + taps[k][:, None] * padded[k : k + count]
    return total


def time_back(padded, taps, count):
    total = jnp.zeros((count,) + padded.shape[1:], jnp.float32)
    for k in range(9):
        total = total + taps[k][:, None] * padded[8 - k : 8 - k + count]
    return total


def time_weight_part(grads, padded, count):
    grads32 = grads.astype(jnp.float32)
    parts = []
    for k in range(9):
        parts.append(jnp.sum(grads32 * padded[k : k + count], axis=(0, 1, 3)))
    return jnp.stack(parts)


def on_device(field, cotangent, space_weight, time_weight):
    frames_here, rows, width_own, cells = field.shape
    start = lax.axis_index("chan") * width_own
    tap_rows = lax.dynamic_slice_in_dim(space_weight, start, width_own, 2)
    tap_cols = lax.dynamic_slice_in_dim(space_weight, start, width_own, 3)
    taps = time_weight.astype(jnp.float32)
    full = widen(field)
    hidden = jnp.zeros(field.shape, jnp.float32)
    for i in range(3):
        for j in range(3):
            hidden = hidden + jnp.einsum(
                "oc,frcw->frow",
                tap_rows[i, j],
                full[:, i : i + rows, :, j : j + cells],
                preferred_element_type=jnp.float32,
            )
    act, pull = jax.vjp(gelu_tanh, hidden)
    acts = act.astype(jnp.bfloat16)
    acts_time = to_time(acts)
    acts_pad = pad_time(acts_time)
    frames = acts_time.shape[0]
    mixed = to_space(time_forward(acts_pad, taps, frames).astype(jnp.bfloat16))
    grad_time = to_time(cotangent)
    back_local = time_back(pad_time(grad_time), taps, frames).astype(jnp.bfloat16)
    time_part = time_weight_part(grad_time, acts_pad, frames)
    back_time = to_space(back_local)
    output = (field.astype(jnp.float32) + mixed.astype(jnp.float32)).astype(jnp.bfloat16)
    back_hidden = pull(back_time.astype(jnp.float32))[0].astype(jnp.bfloat16)
    wide_grad = widen(back_hidden)
    back_field = cotangent.astype(jnp.float32)
    space_rows = []
    for i in range(3):
        inner = []
        for j in range(3):
            back_field = back_field + jnp.einsum(
                "oc,frow->frcw",
                tap_cols[i, j],
                wide_grad[:, 2 - i : 2 - i + rows, :, 2 - j : 2 - j + cells],
                preferred_element_type=jnp.float32,
            )
            inner.append(
                jnp.einsum(
                    "frow,frcw->oc",
                    back_hidden,
                    full[:, i : i + rows, :, j : j + cells],
                    preferred_element_type=jnp.float32,
                )
            )
        space_rows.append(jnp.stack(inner))
    field_grad = back_field.astype(jnp.bfloat16)
    space_part = jnp.stack(space_rows)
    space_total, time_total = lax.psum((space_part, time_part), ("shard", "sub"))
    total_frames = frames_here * lax.axis_size("shard")
    total_rows = rows * lax.axis_size("sub")
    scale = float(total_frames * total_rows * cells) ** (-0.5)
    return (output, field_grad, space_total * scale, time_total * scale)


def solution(mesh):
    placed = (
        P(("groups", "shard"), "sub", "chan", None),
        P(("groups", "shard"), "sub", "chan", None),
        P(),
        P(None, "chan"),
    )
    return jax.shard_map(
        on_device,
        mesh=mesh,
        in_specs=placed,
        out_specs=(
            P(("groups", "shard"), "sub", "chan", None),
            P(("groups", "shard"), "sub", "chan", None),
            P("groups", None, "chan", None),
            P("groups", "chan"),
        ),
        check_vma=False,
    )
```

profile of v0, /device:TPU:0, one launch (start us, length us, event | category | flops | bytes accessed | tf_op | source)
XLA Modules:
  0.0 162.7 jit_solution(8335515254754302777)
XLA Ops:
  7.2 0.9 fusion.95
  8.1 4.9 %collective-permute-start = (bf16[4,1,48,128]{3,2,1,0:T(8,128)(2,1)S(1)}, bf16[4,1,48,128]{3,2,1,0:T(8,128)(2,1)S(1)}, u32[]{:S(2)}, u32[]{:S(2)}) collective-permute-start(bf16[4,1,48,128]{3,2,1,0:T(8,128)(2,1)S(1)} %get-tuple-element.24), channel_id=1, source_target_pairs={{0,2},{1,3},{4,6},{5,7},{8,10},{9,11},{12,14},{13,15},{16,18},{17,... | collective-permute-start | bytes 147464 | tf_op jit(solution)/shard_map/ppermute | solution.py:15
  13.0 1.3 collective-permute-start.1
  14.3 1.6 copy.19
  15.9 4.9 %all-to-all-start.2 = ((bf16[4,4,48,128]{3,2,0,1:T(8,128)(2,1)}), bf16[4,4,48,128]{3,2,0,1:T(8,128)(2,1)S(1)}, u32[]{:S(2)}, u32[]{:S(2)}) async-start(bf16[4,4,48,128]{3,2,0,1:T(8,128)(2,1)} %copy.19), calls=%async_computation.2 | async-start | bytes 393216 | tf_op jit(solution)/shard_map/all_to_all | solution.py:35
  20.9 2.2 %all_gather.6 = bf16[4,6,96,128]{3,2,1,0:T(8,128)(2,1)S(1)} all-gather(bf16[4,6,48,128]{3,2,1,0:T(8,128)(2,1)S(1)} %pad_maximum_fusion), channel_id=1, replica_groups=mesh['groups'=2,'shard'=4,'sub'=2,'chan'=2] {'chan'}, dimensions={2}, use_global_device_ids=true | all-gather | bytes 884736 | tf_op jit(solution)/shard_map/all_gather | solution.py:30
  23.1 0.3 fusion.55
  23.6 0.3 convolution_add_fusion.6
  23.9 0.3 convolution_add_fusion.5
  24.5 0.3 convolution_add_fusion.3
  24.8 3.2 %all-to-all-done.2 = bf16[4,4,48,128]{3,2,0,1:T(8,128)(2,1)S(1)} async-done(((bf16[4,4,48,128]{3,2,0,1:T(8,128)(2,1)}), bf16[4,4,48,128]{3,2,0,1:T(8,128)(2,1)S(1)}, u32[]{:S(2)}, u32[]{:S(2)}) %all-to-all-start.2) | async-done | bytes 196640 | tf_op jit(solution)/shard_map/all_to_all | solution.py:35
  28.1 1.0 fusion.56
  29.1 3.4 %all-to-all-start.3 = ((bf16[16,1,48,128]{3,2,1,0:T(8,128)(2,1)}), bf16[16,1,48,128]{3,2,1,0:T(8,128)(2,1)S(1)}, u32[]{:S(2)}, u32[]{:S(2)}) async-start(bf16[16,1,48,128]{3,2,1,0:T(8,128)(2,1)} %fusion.56), calls=%async_computation.3 | async-start | bytes 393216 | tf_op jit(solution)/shard_map/all_to_all | solution.py:39
  32.4 0.3 convolution_add_fusion.2
  33.0 5.7 %all-to-all-done.3 = bf16[16,1,48,128]{3,2,1,0:T(8,128)(2,1)S(1)} async-done(((bf16[16,1,48,128]{3,2,1,0:T(8,128)(2,1)}), bf16[16,1,48,128]{3,2,1,0:T(8,128)(2,1)S(1)}, u32[]{:S(2)}, u32[]{:S(2)}) %all-to-all-start.3) | async-done | bytes 196640 | tf_op jit(solution)/shard_map/all_to_all | solution.py:39
  38.7 0.6 fusion.26
  39.5 0.3 convolution_bitcast_fusion.11
  39.8 0.3 convolution_bitcast_fusion.12
  40.1 0.2 convolution_bitcast_fusion.13
  40.4 0.3 convolution_bitcast_fusion.14
  40.7 0.3 convolution_bitcast_fusion.15
  41.1 0.2 convolution_bitcast_fusion.16
  41.3 0.3 convolution_bitcast_fusion.17
  41.7 0.3 convolution_bitcast_fusion.9
  42.0 0.7 copy.16
  42.7 3.4 %all-to-all-start = ((bf16[4,4,48,128]{3,2,0,1:T(8,128)(2,1)}), bf16[4,4,48,128]{3,2,0,1:T(8,128)(2,1)S(1)}, u32[]{:S(2)}, u32[]{:S(2)}) async-start(bf16[4,4,48,128]{3,2,0,1:T(8,128)(2,1)} %copy.16), calls=%async_computation | async-start | bytes 393216 | tf_op jit(solution)/shard_map/all_to_all | solution.py:35
  46.1 4.5 %collective-permute-start.2 = (bf16[4,1,48,128]{3,2,1,0:T(8,128)(2,1)S(1)}, bf16[4,1,48,128]{3,2,1,0:T(8,128)(2,1)S(1)}, u32[]{:S(2)}, u32[]{:S(2)}) collective-permute-start(bf16[4,1,48,128]{3,2,1,0:T(8,128)(2,1)S(1)} %get-tuple-element.22), channel_id=1, source_target_pairs={{0,2},{1,3},{4,6},{5,7},{8,10},{9,11},{12,14},{13,15},{16,18},{17,... | collective-permute-start | bytes 147464 | tf_op jit(solution)/shard_map/ppermute | solution.py:15
  50.7 1.3 collective-permute-start.3
  52.0 0.7 pad_maximum_fusion.2
  52.8 3.9 %collective-permute-done.3 = bf16[4,1,48,128]{3,2,1,0:T(8,128)(2,1)S(1)} collective-permute-done((bf16[4,1,48,128]{3,2,1,0:T(8,128)(2,1)S(1)}, bf16[4,1,48,128]{3,2,1,0:T(8,128)(2,1)S(1)}, u32[]{:S(2)}, u32[]{:S(2)}) %collective-permute-start.3) | collective-permute-done | bytes 49184 | tf_op jit(solution)/shard_map/ppermute | solution.py:17
  56.7 2.4 %all_gather.7 = bf16[4,6,96,128]{3,2,1,0:T(8,128)(2,1)S(1)} all-gather(bf16[4,6,48,128]{3,2,1,0:T(8,128)(2,1)S(1)} %pad_maximum_fusion.1), channel_id=1, replica_groups=mesh['groups'=2,'shard'=4,'sub'=2,'chan'=2] {'chan'}, dimensions={2}, use_global_device_ids=true | all-gather | bytes 884736 | tf_op jit(solution)/shard_map/all_gather | solution.py:30
  59.1 0.3 fusion.8
  59.4 0.3 fusion.7
  59.7 0.3 fusion.6
  60.1 0.3 fusion.5
  60.4 0.3 fusion.4
  60.8 0.3 fusion.3
  61.1 0.3 fusion.2
  61.5 0.3 fusion.1
  61.8 1.0 fusion.10
  62.8 63.5 %all-reduce.6.cloned.1.call-done = f32[3,3,48,96]{3,2,1,0:T(8,128)} async-done(((f32[3,3,48,96]{3,2,1,0:T(8,128)}), f32[3,3,48,96]{3,2,1,0:T(8,128)}) %all-reduce.6.cloned.1.call-update) | async-done | bytes 165904 | tf_op jit(solution)/shard_map/psum | solution.py:119
  126.3 1.6 %broadcast_multiply_fusion = f32[3,3,48,96]{3,2,1,0:T(8,128)} fusion(f32[3,3,48,96]{3,2,1,0:T(8,128)} %all-reduce.6.cloned.1.call-done), kind=kLoop, calls=%fused_computation.138 | loop fusion | flops 41472 | bytes 331776 | tf_op jit(solution)/shard_map/mul | solution.py:123
  128.0 1.0 fusion.57
  129.0 0.4 fusion.40
  129.4 3.7 %all-to-all-start.1 = ((bf16[16,1,48,128]{3,2,1,0:T(8,128)(2,1)}), bf16[16,1,48,128]{3,2,1,0:T(8,128)(2,1)S(1)}, u32[]{:S(2)}, u32[]{:S(2)}) async-start(bf16[16,1,48,128]{3,2,1,0:T(8,128)(2,1)} %fusion.57), calls=%async_computation.1 | async-start | bytes 393216 | tf_op jit(solution)/shard_map/all_to_all | solution.py:39
  133.2 21.3 %psum.15 = f32[9,48]{1,0:T(8,128)S(1)} all-reduce(f32[9,48]{1,0:T(8,128)S(1)} %stack.103), channel_id=1, replica_groups=mesh['groups'=2,'shard'=4,'sub'=2,'chan'=2] {'shard','sub'}, use_global_device_ids=true, to_apply=%region_10.11 | all-reduce | flops 432 | bytes 3456 | tf_op jit(solution)/shard_map/psum | solution.py:119
  154.5 0.6 broadcast_multiply_fusion.1
  155.2 0.7 copy.24
  (29 shorter events, 1.3 us)
Async XLA Ops:
  7.2 15.9 %copy-start = (bf16[3,3,96,96]{3,2,1,0:T(8,128)(2,1)S(1)}, bf16[3,3,96,96]{3,2,1,0:T(8,128)(2,1)}, u32[]{:S(2)}) copy-start(bf16[3,3,96,96]{3,2,1,0:T(8,128)(2,1)} %param.6) | copy-start | bytes 497668
  7.2 13.6 %copy-start.1 = (bf16[4,4,48,128]{3,2,1,0:T(8,128)(2,1)S(1)}, bf16[4,4,48,128]{3,2,1,0:T(8,128)(2,1)}, u32[]{:S(2)}) copy-start(bf16[4,4,48,128]{3,2,1,0:T(8,128)(2,1)} %param.4) | copy-start | bytes 589828
  7.2 13.6 %copy-start.3 = (bf16[9,48]{1,0:T(8,128)(2,1)S(1)}, bf16[9,48]{1,0:T(8,128)(2,1)}, u32[]{:S(2)}) copy-start(bf16[9,48]{1,0:T(8,128)(2,1)} %param.7) | copy-start | bytes 2596
  8.1 12.7 %collective-permute-start = (bf16[4,1,48,128]{3,2,1,0:T(8,128)(2,1)S(1)}, bf16[4,1,48,128]{3,2,1,0:T(8,128)(2,1)S(1)}, u32[]{:S(2)}, u32[]{:S(2)}) collective-permute-start(bf16[4,1,48,128]{3,2,1,0:T(8,128)(2,1)S(1)} %get-tuple-element.24), channel_id=1, source_target_pairs={{0,2},{1,3},{4,6},{5,7},{8,10},{9,11},{12,14},{13,15},{16,18},{17,... | collective-permute-start | bytes 147464 | tf_op jit(solution)/shard_map/ppermute | solution.py:15
  13.0 7.8 %collective-permute-start.1 = (bf16[4,1,48,128]{3,2,1,0:T(8,128)(2,1)S(1)}, bf16[4,1,48,128]{3,2,1,0:T(8,128)(2,1)S(1)}, u32[]{:S(2)}, u32[]{:S(2)}) collective-permute-start(bf16[4,1,48,128]{3,2,1,0:T(8,128)(2,1)S(1)} %get-tuple-element.25), channel_id=1, source_target_pairs={{2,0},{3,1},{6,4},{7,5},{10,8},{11,9},{14,12},{15,13},{18,16},{19,... | collective-permute-start | bytes 147464 | tf_op jit(solution)/shard_map/ppermute | solution.py:17
  15.9 12.2 %all-to-all-start.2 = ((bf16[4,4,48,128]{3,2,0,1:T(8,128)(2,1)}), bf16[4,4,48,128]{3,2,0,1:T(8,128)(2,1)S(1)}, u32[]{:S(2)}, u32[]{:S(2)}) async-start(bf16[4,4,48,128]{3,2,0,1:T(8,128)(2,1)} %copy.19), calls=%async_computation.2 | async-start | bytes 393216 | tf_op jit(solution)/shard_map/all_to_all | solution.py:35
  29.1 9.6 %all-to-all-start.3 = ((bf16[16,1,48,128]{3,2,1,0:T(8,128)(2,1)}), bf16[16,1,48,128]{3,2,1,0:T(8,128)(2,1)S(1)}, u32[]{:S(2)}, u32[]{:S(2)}) async-start(bf16[16,1,48,128]{3,2,1,0:T(8,128)(2,1)} %fusion.56), calls=%async_computation.3 | async-start | bytes 393216 | tf_op jit(solution)/shard_map/all_to_all | solution.py:39
  42.7 85.3 %all-to-all-start = ((bf16[4,4,48,128]{3,2,0,1:T(8,128)(2,1)}), bf16[4,4,48,128]{3,2,0,1:T(8,128)(2,1)S(1)}, u32[]{:S(2)}, u32[]{:S(2)}) async-start(bf16[4,4,48,128]{3,2,0,1:T(8,128)(2,1)} %copy.16), calls=%async_computation | async-start | bytes 393216 | tf_op jit(solution)/shard_map/all_to_all | solution.py:35
  46.1 80.3 %all-reduce.6.cloned.1.call-start = ((), (), s32[]{:S(2)}) async-start(), calls=%async_computation.4 | async-start | bytes 442368 | tf_op jit(solution)/shard_map/psum | solution.py:119
  46.1 6.6 %collective-permute-start.2 = (bf16[4,1,48,128]{3,2,1,0:T(8,128)(2,1)S(1)}, bf16[4,1,48,128]{3,2,1,0:T(8,128)(2,1)S(1)}, u32[]{:S(2)}, u32[]{:S(2)}) collective-permute-start(bf16[4,1,48,128]{3,2,1,0:T(8,128)(2,1)S(1)} %get-tuple-element.22), channel_id=1, source_target_pairs={{0,2},{1,3},{4,6},{5,7},{8,10},{9,11},{12,14},{13,15},{16,18},{17,... | collective-permute-start | bytes 147464 | tf_op jit(solution)/shard_map/ppermute | solution.py:15
  50.7 6.0 %collective-permute-start.3 = (bf16[4,1,48,128]{3,2,1,0:T(8,128)(2,1)S(1)}, bf16[4,1,48,128]{3,2,1,0:T(8,128)(2,1)S(1)}, u32[]{:S(2)}, u32[]{:S(2)}) collective-permute-start(bf16[4,1,48,128]{3,2,1,0:T(8,128)(2,1)S(1)} %get-tuple-element.23), channel_id=1, source_target_pairs={{2,0},{3,1},{6,4},{7,5},{10,8},{11,9},{14,12},{15,13},{18,16},{19,... | collective-permute-start | bytes 147464 | tf_op jit(solution)/shard_map/ppermute | solution.py:17
  56.7 2.4 %copy-start.2 = (bf16[4,4,48,128]{3,2,1,0:T(8,128)(2,1)S(1)}, bf16[4,4,48,128]{3,2,1,0:T(8,128)(2,1)}, u32[]{:S(2)}) copy-start(bf16[4,4,48,128]{3,2,1,0:T(8,128)(2,1)} %param.5) | copy-start | bytes 589828
  129.4 25.8 %all-to-all-start.1 = ((bf16[16,1,48,128]{3,2,1,0:T(8,128)(2,1)}), bf16[16,1,48,128]{3,2,1,0:T(8,128)(2,1)S(1)}, u32[]{:S(2)}, u32[]{:S(2)}) async-start(bf16[16,1,48,128]{3,2,1,0:T(8,128)(2,1)} %fusion.57), calls=%async_computation.1 | async-start | bytes 393216 | tf_op jit(solution)/shard_map/all_to_all | solution.py:39
Sparse Core Ops, SparseCore 0:
  52.9 73.4 all-reduce.5
where the time goes:
time: 163 us
  waiting for transfers between devices  76.4 us (47%)
  starting transfers between devices  27.3 us (17%)
  blocking collectives  25.9 us (16%)
  between operations  14.4 us (9%)
  matrix products  9.13 us (6%)
  other arithmetic  5.67 us (3%)
  local copies, waits for them, and re-layouts  3.97 us (2%)
    psum x1, waiting for transfers between devices, on_device(): lax.psum((space_part, time_part), ('shard', 'sub'))  63.5 us
    psum x1, blocking collectives, on_device(): lax.psum((space_part, time_part), ('shard', 'sub'))  21.3 us
    ppermute x2, starting transfers between devices, with_halo(): lax.ppermute(tail, axis, [(i, (i + 1) % count) for i in range(ends)])  9.39 us
    all_to_all x2, starting transfers between devices, to_time(): lax.all_to_all(values, 'shard', split_axis=1, concat_axis=0, tiled=True)  8.24 us
    all_to_all x2, starting transfers between devices, to_space(): lax.all_to_all(values, 'shard', split_axis=0, concat_axis=1, tiled=True)  7.02 us
    all_to_all x2, waiting for transfers between devices, to_space(): lax.all_to_all(values, 'shard', split_axis=0, concat_axis=1, tiled=True)  5.68 us
    all_gather x2, blocking collectives, widen(): gathered = lax.all_gather(rimmed, 'chan', axis=2, tiled=True)  4.59 us
    ppermute x2, waiting for transfers between devices, with_halo(): lax.ppermute(head, axis, [((i + 1) % count, i) for i in range(ends)])  3.9 us
  transfers between devices with their start and end apart: 9, of which 4 were waited for; matrix products, arithmetic and copies ran while one was open for 7% of the time, Pallas kernels for 0%

commit v1 on v0

--- a/solution.py
+++ b/solution.py
@@ -2,6 +2,10 @@
 import jax.numpy as jnp
 from jax import lax
 from jax.sharding import PartitionSpec as P
+
+
+def refer_spans(xin):
+    return lax.psum(lax.psum(xin, "sub"), "shard")
 
 
 def with_halo(cells, sides, width):
@@ -116,7 +120,7 @@
         space_rows.append(jnp.stack(inner))
     field_grad = back_field.astype(jnp.bfloat16)
     space_part = jnp.stack(space_rows)
-    space_total, time_total = lax.psum((space_part, time_part), ("shard", "sub"))
+    space_total, time_total = refer_spans((space_part, time_part))
     total_frames = frames_here * lax.axis_size("shard")
     total_rows = rows * lax.axis_size("sub")
     scale = float(total_frames * total_rows * cells) ** (-0.5)

time: 163 us -> 126 us (0.77)
  waiting for transfers between devices: 76.4 us -> 43.5 us
  blocking collectives: 25.9 us -> 21.4 us
    psum x1 -> x2, waiting for transfers between devices: 63.5 us -> 30.7 us  [refer_spans(): return lax.psum(lax.psum(xin, 'sub'), 'shard')]
    psum x1 -> x2, blocking collectives: 21.3 us -> 16.8 us  [refer_spans(): return lax.psum(lax.psum(xin, 'sub'), 'shard')]
  transfers between devices with their start and end apart: 9 -> 10, of which waited for: 4 -> 5; matrix products, arithmetic and copies ran while one was open for 7% -> 10% of each run, Pallas kernels for 0% -> 0%
where the time goes in v1:
time: 126 us; the launch traced here: 125 us
  waiting for transfers between devices  43.5 us (35%)
  starting transfers between devices  27 us (21%)
  blocking collectives  21.4 us (17%)
  between operations  14.5 us (12%)
  matrix products  9.13 us (7%)
  other arithmetic  5.67 us (4%)
  local copies, waits for them, and re-layouts  3.97 us (3%)
    psum x2, waiting for transfers between devices, refer_spans(): return lax.psum(lax.psum(xin, 'sub'), 'shard')  30.7 us
    psum x2, blocking collectives, refer_spans(): return lax.psum(lax.psum(xin, 'sub'), 'shard')  16.8 us
    ppermute x2, starting transfers between devices, with_halo(): lax.ppermute(tail, axis, [(i, (i + 1) % count) for i in range(ends)])  9.39 us
    all_to_all x2, starting transfers between devices, to_time(): lax.all_to_all(values, 'shard', split_axis=1, concat_axis=0, tiled=True)  8.24 us
    all_to_all x2, starting transfers between devices, to_space(): lax.all_to_all(values, 'shard', split_axis=0, concat_axis=1, tiled=True)  6.74 us
    all_to_all x2, waiting for transfers between devices, to_space(): lax.all_to_all(values, 'shard', split_axis=0, concat_axis=1, tiled=True)  5.68 us
    all_gather x2, blocking collectives, widen(): gathered = lax.all_gather(rimmed, 'chan', axis=2, tiled=True)  4.59 us
    ppermute x2, waiting for transfers between devices, with_halo(): lax.ppermute(head, axis, [((i + 1) % count, i) for i in range(ends)])  3.85 us
  transfers between devices with their start and end apart: 10, of which 5 were waited for; matrix products, arithmetic and copies ran while one was open for 10% of the time, Pallas kernels for 0%

profile of v1, /device:TPU:0, one launch (start us, length us, event | category | flops | bytes accessed | tf_op | source)
XLA Modules:
  0.0 125.2 jit_solution(15886079160552467753)
XLA Ops:
  7.2 0.9 fusion.95
  8.1 4.9 %collective-permute-start = (bf16[4,1,48,128]{3,2,1,0:T(8,128)(2,1)S(1)}, bf16[4,1,48,128]{3,2,1,0:T(8,128)(2,1)S(1)}, u32[]{:S(2)}, u32[]{:S(2)}) collective-permute-start(bf16[4,1,48,128]{3,2,1,0:T(8,128)(2,1)S(1)} %get-tuple-element.24), channel_id=1, source_target_pairs={{0,2},{1,3},{4,6},{5,7},{8,10},{9,11},{12,14},{13,15},{16,18},{17,... | collective-permute-start | bytes 147464 | tf_op jit(solution)/shard_map/ppermute | solution.py:19
  13.0 1.3 %collective-permute-start.1 = (bf16[4,1,48,128]{3,2,1,0:T(8,128)(2,1)S(1)}, bf16[4,1,48,128]{3,2,1,0:T(8,128)(2,1)S(1)}, u32[]{:S(2)}, u32[]{:S(2)}) collective-permute-start(bf16[4,1,48,128]{3,2,1,0:T(8,128)(2,1)S(1)} %get-tuple-element.25), channel_id=1, source_target_pairs={{2,0},{3,1},{6,4},{7,5},{10,8},{11,9},{14,12},{15,13},{18,16},{19,... | collective-permute-start | bytes 147464 | tf_op jit(solution)/shard_map/ppermute | solution.py:21
  14.3 1.6 %copy.19 = bf16[4,4,48,128]{3,2,0,1:T(8,128)(2,1)} copy(bf16[4,4,48,128]{3,2,1,0:T(8,128)(2,1)} %param.5) | data formatting | bytes 393216 | tf_op args[1]
  15.9 4.9 %all-to-all-start.2 = ((bf16[4,4,48,128]{3,2,0,1:T(8,128)(2,1)}), bf16[4,4,48,128]{3,2,0,1:T(8,128)(2,1)S(1)}, u32[]{:S(2)}, u32[]{:S(2)}) async-start(bf16[4,4,48,128]{3,2,0,1:T(8,128)(2,1)} %copy.19), calls=%async_computation.2 | async-start | bytes 393216 | tf_op jit(solution)/shard_map/all_to_all | solution.py:39
  20.9 2.2 %all_gather.6 = bf16[4,6,96,128]{3,2,1,0:T(8,128)(2,1)S(1)} all-gather(bf16[4,6,48,128]{3,2,1,0:T(8,128)(2,1)S(1)} %pad_maximum_fusion), channel_id=1, replica_groups=mesh['groups'=2,'shard'=4,'sub'=2,'chan'=2] {'chan'}, dimensions={2}, use_global_device_ids=true | all-gather | bytes 884736 | tf_op jit(solution)/shard_map/all_gather | solution.py:34
  23.1 0.3 fusion.55
  23.6 0.3 convolution_add_fusion.6
  23.9 0.3 convolution_add_fusion.5
  24.5 0.3 convolution_add_fusion.3
  24.8 3.2 %all-to-all-done.2 = bf16[4,4,48,128]{3,2,0,1:T(8,128)(2,1)S(1)} async-done(((bf16[4,4,48,128]{3,2,0,1:T(8,128)(2,1)}), bf16[4,4,48,128]{3,2,0,1:T(8,128)(2,1)S(1)}, u32[]{:S(2)}, u32[]{:S(2)}) %all-to-all-start.2) | async-done | bytes 196640 | tf_op jit(solution)/shard_map/all_to_all | solution.py:39
  28.1 1.0 fusion.56
  29.1 3.4 %all-to-all-start.3 = ((bf16[16,1,48,128]{3,2,1,0:T(8,128)(2,1)}), bf16[16,1,48,128]{3,2,1,0:T(8,128)(2,1)S(1)}, u32[]{:S(2)}, u32[]{:S(2)}) async-start(bf16[16,1,48,128]{3,2,1,0:T(8,128)(2,1)} %fusion.56), calls=%async_computation.3 | async-start | bytes 393216 | tf_op jit(solution)/shard_map/all_to_all | solution.py:43
  32.4 0.3 convolution_add_fusion.2
  33.0 5.7 %all-to-all-done.3 = bf16[16,1,48,128]{3,2,1,0:T(8,128)(2,1)S(1)} async-done(((bf16[16,1,48,128]{3,2,1,0:T(8,128)(2,1)}), bf16[16,1,48,128]{3,2,1,0:T(8,128)(2,1)S(1)}, u32[]{:S(2)}, u32[]{:S(2)}) %all-to-all-start.3) | async-done | bytes 196640 | tf_op jit(solution)/shard_map/all_to_all | solution.py:43
  38.7 0.6 fusion.26
  39.5 0.3 convolution_bitcast_fusion.11
  39.8 0.3 convolution_bitcast_fusion.12
  40.4 0.3 convolution_bitcast_fusion.14
  40.7 0.3 convolution_bitcast_fusion.15
  41.3 0.3 convolution_bitcast_fusion.17
  41.7 0.3 convolution_bitcast_fusion.9
  42.0 0.7 copy.16
  42.7 3.4 %all-to-all-start = ((bf16[4,4,48,128]{3,2,0,1:T(8,128)(2,1)}), bf16[4,4,48,128]{3,2,0,1:T(8,128)(2,1)S(1)}, u32[]{:S(2)}, u32[]{:S(2)}) async-start(bf16[4,4,48,128]{3,2,0,1:T(8,128)(2,1)} %copy.16), calls=%async_computation | async-start | bytes 393216 | tf_op jit(solution)/shard_map/all_to_all | solution.py:39
  46.1 4.5 %collective-permute-start.2 = (bf16[4,1,48,128]{3,2,1,0:T(8,128)(2,1)S(1)}, bf16[4,1,48,128]{3,2,1,0:T(8,128)(2,1)S(1)}, u32[]{:S(2)}, u32[]{:S(2)}) collective-permute-start(bf16[4,1,48,128]{3,2,1,0:T(8,128)(2,1)S(1)} %get-tuple-element.22), channel_id=1, source_target_pairs={{0,2},{1,3},{4,6},{5,7},{8,10},{9,11},{12,14},{13,15},{16,18},{17,... | collective-permute-start | bytes 147464 | tf_op jit(solution)/shard_map/ppermute | solution.py:19
  50.7 1.3 %collective-permute-start.3 = (bf16[4,1,48,128]{3,2,1,0:T(8,128)(2,1)S(1)}, bf16[4,1,48,128]{3,2,1,0:T(8,128)(2,1)S(1)}, u32[]{:S(2)}, u32[]{:S(2)}) collective-permute-start(bf16[4,1,48,128]{3,2,1,0:T(8,128)(2,1)S(1)} %get-tuple-element.23), channel_id=1, source_target_pairs={{2,0},{3,1},{6,4},{7,5},{10,8},{11,9},{14,12},{15,13},{18,16},{19,... | collective-permute-start | bytes 147464 | tf_op jit(solution)/shard_map/ppermute | solution.py:21
  52.0 0.7 pad_maximum_fusion.2
  52.8 3.9 %collective-permute-done.3 = bf16[4,1,48,128]{3,2,1,0:T(8,128)(2,1)S(1)} collective-permute-done((bf16[4,1,48,128]{3,2,1,0:T(8,128)(2,1)S(1)}, bf16[4,1,48,128]{3,2,1,0:T(8,128)(2,1)S(1)}, u32[]{:S(2)}, u32[]{:S(2)}) %collective-permute-start.3) | collective-permute-done | bytes 49184 | tf_op jit(solution)/shard_map/ppermute | solution.py:21
  56.7 2.4 %all_gather.7 = bf16[4,6,96,128]{3,2,1,0:T(8,128)(2,1)S(1)} all-gather(bf16[4,6,48,128]{3,2,1,0:T(8,128)(2,1)S(1)} %pad_maximum_fusion.1), channel_id=1, replica_groups=mesh['groups'=2,'shard'=4,'sub'=2,'chan'=2] {'chan'}, dimensions={2}, use_global_device_ids=true | all-gather | bytes 884736 | tf_op jit(solution)/shard_map/all_gather | solution.py:34
  59.1 0.3 fusion.8
  59.4 0.3 fusion.7
  59.7 0.3 fusion.6
  60.1 0.3 fusion.5
  60.4 0.3 fusion.4
  60.8 0.3 fusion.3
  61.1 0.3 fusion.2
  61.5 0.3 fusion.1
  61.8 1.0 fusion.10
  62.8 15.4 %all-reduce.7.cloned.1.call-done = f32[3,3,48,96]{3,2,1,0:T(8,128)} async-done(((f32[3,3,48,96]{3,2,1,0:T(8,128)}), f32[3,3,48,96]{3,2,1,0:T(8,128)}) %all-reduce.7.cloned.1.call-update) | async-done | bytes 165904 | tf_op jit(solution)/shard_map/psum | solution.py:8
  78.2 1.0 fusion.57
  79.3 0.4 fusion.40
  79.8 5.0 %psum.30 = f32[9,48]{1,0:T(8,128)S(1)} all-reduce(f32[9,48]{1,0:T(8,128)S(1)} %stack.103), channel_id=1, replica_groups=mesh['groups'=2,'shard'=4,'sub'=2,'chan'=2] {'sub'}, use_global_device_ids=true, to_apply=%region_11.12 | all-reduce | flops 432 | bytes 3456 | tf_op jit(solution)/shard_map/psum | solution.py:8
  84.8 11.8 %psum.31 = f32[9,48]{1,0:T(8,128)S(1)} all-reduce(f32[9,48]{1,0:T(8,128)S(1)} %psum.30), channel_id=1, replica_groups=mesh['groups'=2,'shard'=4,'sub'=2,'chan'=2] {'shard'}, use_global_device_ids=true, to_apply=%region_12.13 | all-reduce | flops 432 | bytes 3456 | tf_op jit(solution)/shard_map/psum | solution.py:8
  96.7 3.4 %all-to-all-start.1 = ((bf16[16,1,48,128]{3,2,1,0:T(8,128)(2,1)}), bf16[16,1,48,128]{3,2,1,0:T(8,128)(2,1)S(1)}, u32[]{:S(2)}, u32[]{:S(2)}) async-start(bf16[16,1,48,128]{3,2,1,0:T(8,128)(2,1)} %fusion.57), calls=%async_computation.1 | async-start | bytes 393216 | tf_op jit(solution)/shard_map/all_to_all | solution.py:43
  100.1 0.6 broadcast_multiply_fusion.1
  100.7 15.3 %all-reduce.9.cloned.1.call-done = f32[3,3,48,96]{3,2,1,0:T(8,128)} async-done(((f32[3,3,48,96]{3,2,1,0:T(8,128)}), f32[3,3,48,96]{3,2,1,0:T(8,128)}) %all-reduce.9.cloned.1.call-update) | async-done | bytes 165904 | tf_op jit(solution)/shard_map/psum | solution.py:8
  116.0 1.6 %broadcast_multiply_fusion = f32[3,3,48,96]{3,2,1,0:T(8,128)} fusion(f32[3,3,48,96]{3,2,1,0:T(8,128)} %all-reduce.9.cloned.1.call-done), kind=kLoop, calls=%fused_computation.138 | loop fusion | flops 41472 | bytes 331776 | tf_op jit(solution)/shard_map/mul | solution.py:127
  117.7 0.7 copy.24
  (33 shorter events, 1.8 us)
Async XLA Ops:
  7.2 15.9 %copy-start = (bf16[3,3,96,96]{3,2,1,0:T(8,128)(2,1)S(1)}, bf16[3,3,96,96]{3,2,1,0:T(8,128)(2,1)}, u32[]{:S(2)}) copy-start(bf16[3,3,96,96]{3,2,1,0:T(8,128)(2,1)} %param.6) | copy-start | bytes 497668
  7.2 13.6 %copy-start.1 = (bf16[4,4,48,128]{3,2,1,0:T(8,128)(2,1)S(1)}, bf16[4,4,48,128]{3,2,1,0:T(8,128)(2,1)}, u32[]{:S(2)}) copy-start(bf16[4,4,48,128]{3,2,1,0:T(8,128)(2,1)} %param.4) | copy-start | bytes 589828
  7.2 13.6 %copy-start.3 = (bf16[9,48]{1,0:T(8,128)(2,1)S(1)}, bf16[9,48]{1,0:T(8,128)(2,1)}, u32[]{:S(2)}) copy-start(bf16[9,48]{1,0:T(8,128)(2,1)} %param.7) | copy-start | bytes 2596
  8.1 12.7 %collective-permute-start = (bf16[4,1,48,128]{3,2,1,0:T(8,128)(2,1)S(1)}, bf16[4,1,48,128]{3,2,1,0:T(8,128)(2,1)S(1)}, u32[]{:S(2)}, u32[]{:S(2)}) collective-permute-start(bf16[4,1,48,128]{3,2,1,0:T(8,128)(2,1)S(1)} %get-tuple-element.24), channel_id=1, source_target_pairs={{0,2},{1,3},{4,6},{5,7},{8,10},{9,11},{12,14},{13,15},{16,18},{17,... | collective-permute-start | bytes 147464 | tf_op jit(solution)/shard_map/ppermute | solution.py:19
  13.0 7.8 %collective-permute-start.1 = (bf16[4,1,48,128]{3,2,1,0:T(8,128)(2,1)S(1)}, bf16[4,1,48,128]{3,2,1,0:T(8,128)(2,1)S(1)}, u32[]{:S(2)}, u32[]{:S(2)}) collective-permute-start(bf16[4,1,48,128]{3,2,1,0:T(8,128)(2,1)S(1)} %get-tuple-element.25), channel_id=1, source_target_pairs={{2,0},{3,1},{6,4},{7,5},{10,8},{11,9},{14,12},{15,13},{18,16},{19,... | collective-permute-start | bytes 147464 | tf_op jit(solution)/shard_map/ppermute | solution.py:21
  15.9 12.2 %all-to-all-start.2 = ((bf16[4,4,48,128]{3,2,0,1:T(8,128)(2,1)}), bf16[4,4,48,128]{3,2,0,1:T(8,128)(2,1)S(1)}, u32[]{:S(2)}, u32[]{:S(2)}) async-start(bf16[4,4,48,128]{3,2,0,1:T(8,128)(2,1)} %copy.19), calls=%async_computation.2 | async-start | bytes 393216 | tf_op jit(solution)/shard_map/all_to_all | solution.py:39
  29.1 9.6 %all-to-all-start.3 = ((bf16[16,1,48,128]{3,2,1,0:T(8,128)(2,1)}), bf16[16,1,48,128]{3,2,1,0:T(8,128)(2,1)S(1)}, u32[]{:S(2)}, u32[]{:S(2)}) async-start(bf16[16,1,48,128]{3,2,1,0:T(8,128)(2,1)} %fusion.56), calls=%async_computation.3 | async-start | bytes 393216 | tf_op jit(solution)/shard_map/all_to_all | solution.py:43
  42.7 35.5 %all-to-all-start = ((bf16[4,4,48,128]{3,2,0,1:T(8,128)(2,1)}), bf16[4,4,48,128]{3,2,0,1:T(8,128)(2,1)S(1)}, u32[]{:S(2)}, u32[]{:S(2)}) async-start(bf16[4,4,48,128]{3,2,0,1:T(8,128)(2,1)} %copy.16), calls=%async_computation | async-start | bytes 393216 | tf_op jit(solution)/shard_map/all_to_all | solution.py:39
  46.1 32.1 %all-reduce.7.cloned.1.call-start = ((), (), s32[]{:S(2)}) async-start(), calls=%async_computation.4 | async-start | bytes 442368 | tf_op jit(solution)/shard_map/psum | solution.py:8
  46.1 6.7 %collective-permute-start.2 = (bf16[4,1,48,128]{3,2,1,0:T(8,128)(2,1)S(1)}, bf16[4,1,48,128]{3,2,1,0:T(8,128)(2,1)S(1)}, u32[]{:S(2)}, u32[]{:S(2)}) collective-permute-start(bf16[4,1,48,128]{3,2,1,0:T(8,128)(2,1)S(1)} %get-tuple-element.22), channel_id=1, source_target_pairs={{0,2},{1,3},{4,6},{5,7},{8,10},{9,11},{12,14},{13,15},{16,18},{17,... | collective-permute-start | bytes 147464 | tf_op jit(solution)/shard_map/ppermute | solution.py:19
  50.7 6.0 %collective-permute-start.3 = (bf16[4,1,48,128]{3,2,1,0:T(8,128)(2,1)S(1)}, bf16[4,1,48,128]{3,2,1,0:T(8,128)(2,1)S(1)}, u32[]{:S(2)}, u32[]{:S(2)}) collective-permute-start(bf16[4,1,48,128]{3,2,1,0:T(8,128)(2,1)S(1)} %get-tuple-element.23), channel_id=1, source_target_pairs={{2,0},{3,1},{6,4},{7,5},{10,8},{11,9},{14,12},{15,13},{18,16},{19,... | collective-permute-start | bytes 147464 | tf_op jit(solution)/shard_map/ppermute | solution.py:21
  52.7 63.2 %all-reduce.9.cloned.1.call-start = ((), (), s32[]{:S(2)}) async-start(), calls=%async_computation.5 | async-start | bytes 442368 | tf_op jit(solution)/shard_map/psum | solution.py:8
  56.7 2.4 %copy-start.2 = (bf16[4,4,48,128]{3,2,1,0:T(8,128)(2,1)S(1)}, bf16[4,4,48,128]{3,2,1,0:T(8,128)(2,1)}, u32[]{:S(2)}) copy-start(bf16[4,4,48,128]{3,2,1,0:T(8,128)(2,1)} %param.5) | copy-start | bytes 589828
  96.7 20.9 %all-to-all-start.1 = ((bf16[16,1,48,128]{3,2,1,0:T(8,128)(2,1)}), bf16[16,1,48,128]{3,2,1,0:T(8,128)(2,1)S(1)}, u32[]{:S(2)}, u32[]{:S(2)}) async-start(bf16[16,1,48,128]{3,2,1,0:T(8,128)(2,1)} %fusion.57), calls=%async_computation.1 | async-start | bytes 393216 | tf_op jit(solution)/shard_map/all_to_all | solution.py:43
Sparse Core Ops, SparseCore 0:
  52.9 25.2 all-reduce.6
  80.5 35.3 all-reduce.8
